TPU v7x, 512 devices: a whole 4x8x8 slice. The times are simulated.
512 devices in a mesh: seq: 64 (over y, z), tp: 8 (over x, core).
Axes of the slice: x: 4, y: 8, z: 8, core: 2. Of those that a mesh axis runs over, the one named last changes fastest.
Arguments:
- queries: bfloat16 [16384, 8192], P('seq', 'tp'), may hold values from -12 to 12
- kv_rows: bfloat16 [16384, 2048], P('seq', 'tp'), may hold values from -6 to 6
- vertical: int32 [64, 32], replicated, may hold values from 0 to 255, as said below
- slash: int32 [64, 8], replicated, may hold values from 0 to 11, as said below
Outputs:
- attended: bfloat16 [16384, 8192], P(('seq', 'tp'))
Inputs may be any that keep to these rules, and one draw needn't show every extreme that they name: `vertical`: each row lists 32 distinct blocks in rising order and includes block 0 and block 255. The heads that share one key-value head list together exactly 48 distinct blocks. `slash`: each row lists 8 distinct offsets in rising order, the first 0 and the last 11.
All inputs are finite; a program needn't handle non-finite values.
Results may differ from a plain program's by a relative error of at most 0.0045.
Values may be sent and summed in bfloat16 or wider, within the bound.
A program may use at most 64 MiB of HBM per device.

v0:
```python
import jax
import jax.numpy as jnp
from jax import lax
from jax.sharding import PartitionSpec as P

HEAD_SIZE = 128
BLK = 64


def as_sent(array):

    def short(part):
        return part.astype(jnp.bfloat16) if part.dtype == jnp.float32 else part

    return jax.tree.map(short, array)


def key_mask(bids, vertical_row, srow):
    dist = bids[:, None] - vertical_row[None, :]
    hit = jnp.any(dist[:, :, None] == srow[None, None, :], axis=2)
    live_v = jnp.logical_and(dist >= 0, jnp.logical_not(hit))
    live_s = bids[:, None] - srow[None, :] >= 0
    live = jnp.concatenate([live_v, live_s], axis=1)
    diag = jnp.concatenate([jnp.zeros(vertical_row.shape, bool), srow == 0])
    rows = jnp.arange(BLK, dtype=jnp.int32)
    lower = rows[None, :] <= rows[:, None]
    return live[:, None, :, None] & (
        jnp.logical_not(diag)[None, None, :, None] | lower[None, :, None, :]
    )


def attend(query_block, vert_block, slash_block, bids, vertical_row, srow):
    count_v = vert_block.shape[0]
    scale = 1.0 / HEAD_SIZE**0.5
    logit_vert = jnp.einsum(
        "unz,syz->unsy",
        query_block,
        vert_block[..., :HEAD_SIZE],
        preferred_element_type=jnp.float32,
    )
    logit_slash = jnp.einsum(
        "unz,suyz->unsy",
        query_block,
        slash_block[..., :HEAD_SIZE],
        preferred_element_type=jnp.float32,
    )
    logit_matrix = jnp.concatenate([logit_vert, logit_slash], axis=2) * scale
    mask = key_mask(bids, vertical_row, srow)
    logit_matrix = jnp.where(mask, logit_matrix, -1e30)
    top = jnp.max(logit_matrix, axis=(2, 3), keepdims=True)
    weights = jnp.where(mask, jnp.exp(logit_matrix - top), 0.0)
    total = jnp.sum(weights, axis=(2, 3))
    probabilities = weights.astype(jnp.bfloat16)
    weighted_sum = jnp.einsum(
        "unsy,syd->und",
        probabilities[:, :, :count_v],
        vert_block[..., HEAD_SIZE:],
        preferred_element_type=jnp.float32,
    )
    weighted_sum = weighted_sum + jnp.einsum(
        "unsy,suyd->und",
        probabilities[:, :, count_v:],
        slash_block[..., HEAD_SIZE:],
        preferred_element_type=jnp.float32,
    )
    return (weighted_sum / total[..., None]).astype(jnp.bfloat16)


def slash_slices(table, starts, key_value_head, block_list):
    pieces = []
    for index in range(starts.shape[0]):
        piece = lax.dynamic_slice(
            table,
            (starts[index], 0, key_value_head, 0),
            (block_list, table.shape[1], 1, table.shape[3]),
        )
        pieces.append(piece[:, :, 0])
    return jnp.stack(pieces, axis=0)


def per_device(queries, kv_rows, vertical, slash):
    tok = queries.shape[0]
    n_tp = lax.axis_size("tp")
    heads_loc = vertical.shape[0] // n_tp
    kv_loc = kv_rows.shape[1] // (2 * HEAD_SIZE)
    group = heads_loc // kv_loc
    block_list = tok // BLK
    seq_pos = lax.axis_index("seq")
    tp_pos = lax.axis_index("tp")
    my_vert = lax.dynamic_slice_in_dim(vertical, tp_pos * heads_loc, heads_loc, 0)
    my_slash = lax.dynamic_slice_in_dim(slash, tp_pos * heads_loc, heads_loc, 0)
    first = seq_pos * block_list
    bids = first + jnp.arange(block_list, dtype=jnp.int32)
    full = lax.all_gather(kv_rows, "seq", axis=0, tiled=True)
    index_table = full.reshape(full.shape[0] // BLK, BLK, kv_loc, 2 * HEAD_SIZE)
    front = 3 * block_list
    padded = jnp.concatenate(
        [jnp.zeros((front, BLK, kv_loc, 2 * HEAD_SIZE), index_table.dtype), index_table], axis=0
    )

    def gather_rows(key_value_head, vertical_row, srow):
        vert_block = index_table[vertical_row, :, key_value_head]
        starts = first + front - srow
        return (vert_block, slash_slices(padded, starts, key_value_head, block_list))

    qheads = jnp.transpose(queries.reshape(block_list, BLK, heads_loc, HEAD_SIZE), (2, 0, 1, 3))

    def one_head(item):
        query_block, vertical_row, srow, key_value_head = item
        vert_block, slash_block = gather_rows(key_value_head, vertical_row, srow)
        return attend(query_block, vert_block, slash_block, bids, vertical_row, srow)

    owners = jnp.arange(heads_loc, dtype=jnp.int32) // group
    outputs = lax.map(one_head, (qheads, my_vert, my_slash, owners))
    attn = jnp.transpose(outputs, (1, 2, 0, 3)).reshape(tok, heads_loc * HEAD_SIZE)
    return lax.all_to_all(as_sent(attn), "tp", split_axis=0, concat_axis=1, tiled=True).astype(
        attn.dtype
    )


def solution(mesh):
    return jax.shard_map(
        per_device,
        mesh=mesh,
        in_specs=(P("seq", "tp"), P("seq", "tp"), P(), P()),
        out_specs=P(("seq", "tp"), None),
        check_vma=False,
    )
```

profile of v0, /device:TPU:1, one launch (start us, length us, event | category | flops | bytes accessed | tf_op | source)
XLA Modules:
  0.0 460.2 jit_solution(17042066455035108971)
XLA Ops:
  8.3 1.1 copy.41
  9.4 0.9 copy.29
  10.4 104.9 %all-gather.2.cloned.1.call-done = bf16[16384,256]{1,0:T(8,128)(2,1)} async-done(((bf16[256,256]{1,0:T(8,128)(2,1)}), bf16[16384,256]{1,0:T(8,128)(2,1)}) %all-gather.2.cloned.1.call-update) | async-done | bytes 8388624 | tf_op jit(solution)/shard_map/all_gather | solution.py:94
  115.2 8.4 %concatenate.19 = bf16[268,64,1,256]{3,1,0,2:T(8,128)(2,1)} pad(bf16[256,64,1,256]{3,1,0,2:T(8,128)(2,1)} %bitcast.144, bf16[]{:T(256)} %constant.98.clone.1), padding=12_0x0_0x0_0x0_0 | pad | bytes 17170434 | tf_op jit(solution)/shard_map/concatenate | solution.py:97
  123.7 313.1 %while.13 = (s32[]{:T(128)}, bf16[8,4,64,128]{3,2,1,0:T(8,128)(2,1)}, s32[8,32]{1,0:T(8,128)S(1)}, s32[8,8]{1,0:T(8,128)S(1)}, bf16[8,4,64,128]{3,2,1,0:T(8,128)...) while((s32[]{:T(128)}, ...), condition=%wide.region_4.5_spmd.clone, body=%wide.region_0.4_spmd.clone.sunk | while | flops 344332768 | bytes 21678552 | solution.py:114
  129.1 0.9 bitcast_dynamic-update-slice_fusion.17
  131.7 0.9 bitcast_dynamic-update-slice_fusion.18
  134.6 0.9 bitcast_dynamic-update-slice_fusion.19
  137.6 0.9 bitcast_dynamic-update-slice_fusion.20
  140.2 0.9 bitcast_dynamic-update-slice_fusion.21
  143.0 0.9 bitcast_dynamic-update-slice_fusion.22
  145.8 0.9 bitcast_dynamic-update-slice_fusion.23
  146.8 1.1 fusion.51
  150.7 4.0 gather_fusion
  154.7 1.6 fusion.53
  156.6 1.4 fusion.55
  158.1 3.0 fusion.56
  161.8 1.0 fusion.57
  185.9 1.1 fusion.51
  189.9 4.0 gather_fusion
  193.9 1.6 fusion.53
  195.8 1.4 fusion.55
  197.2 3.0 fusion.56
  201.0 1.0 fusion.57
  225.0 1.1 fusion.51
  229.0 4.0 gather_fusion
  233.0 1.6 fusion.53
  234.9 1.4 fusion.55
  236.3 3.0 fusion.56
  240.1 1.0 fusion.57
  246.5 0.9 bitcast_dynamic-update-slice_fusion.17
  264.2 1.1 fusion.51
  268.1 4.0 gather_fusion
  272.1 1.6 fusion.53
  274.0 1.4 fusion.55
  275.5 3.0 fusion.56
  279.2 1.0 fusion.57
  296.7 0.9 bitcast_dynamic-update-slice_fusion.21
  303.3 1.1 fusion.51
  307.3 4.0 gather_fusion
  311.3 1.6 fusion.53
  313.2 1.4 fusion.55
  314.6 3.0 fusion.56
  318.4 1.0 fusion.57
  342.4 1.1 fusion.51
  346.4 4.0 gather_fusion
  350.4 1.6 fusion.53
  352.3 1.4 fusion.55
  353.7 3.0 fusion.56
  357.5 1.0 fusion.57
  381.6 1.1 fusion.51
  385.5 4.0 gather_fusion
  389.6 1.6 fusion.53
  391.4 1.4 fusion.55
  392.9 3.0 fusion.56
  396.6 1.0 fusion.57
  420.7 1.1 fusion.51
  424.7 4.0 gather_fusion
  428.7 1.6 fusion.53
  430.6 1.4 fusion.55
  432.0 3.0 fusion.56
  435.8 1.0 fusion.57
  436.8 1.4 copy.31
  438.4 14.1 %all_to_all.19 = bf16[8,32,1024]{2,1,0:T(8,128)(2,1)S(1)} all-to-all(bf16[8,32,1024]{2,1,0:T(8,128)(2,1)S(1)} %all_to_all.14), channel_id=1, replica_groups=mesh['seq'=64,'tp'=8] {'tp'}, dimensions={0} | all-to-all | bytes 1048576 | tf_op jit(solution)/shard_map/all_to_all | solution.py:116
  (196 shorter events, 75.2 us)
Async XLA Ops:
  6.5 0.7 copy-start
  6.5 108.7 %all-gather.2.cloned.1.call-start = ((), (), s32[]{:S(2)}) async-start(), calls=%async_computation.1 | async-start | bytes 8519680 | tf_op jit(solution)/shard_map/all_gather | solution.py:94
Sparse Core Ops, SparseCore 0:
  10.4 104.8 all-gather.1
where the time goes:
time: 465 us; the launch traced here: 460 us
  loops' own time  135 us (29%)
  local copies, waits for them, and re-layouts  115 us (25%)
  waiting for transfers between devices  106 us (23%)
  other arithmetic  41.5 us (9%)
  matrix products  35.1 us (8%)
  blocking collectives  14.1 us (3%)
  between operations  13.4 us (3%)
    another operation x1, loops' own time, per_device(): outputs = lax.map(one_head, (qheads, my_vert, my_slash, owners))  135 us
    all_gather x1, waiting for transfers between devices, per_device(): full = lax.all_gather(kv_rows, 'seq', axis=0, tiled=True)  105 us
    while x56, local copies, waits for them, and re-layouts  51.4 us
    gather x8, local copies, waits for them, and re-layouts, gather_rows(): vert_block = index_table[vertical_row, :, key_value_head]  32 us
    reduce_sum x8, other arithmetic, attend(): total = jnp.sum(weights, axis=(2, 3))  24.2 us
    all_to_all x1, blocking collectives, per_device(): lax.all_to_all(as_sent(attn), 'tp', split_axis=0, concat_axis=1, tiled=True)  14.1 us
    dot_general x8, matrix products, attend(): jnp.einsum('unz,syz->unsy', query_block, vert_block[..., :HEAD_SIZE], pre...  12.5 us
    reduce_max x8, other arithmetic, attend(): top = jnp.max(logit_matrix, axis=(2, 3), keepdims=True)  11.5 us
  transfers between devices with their start and end apart: 1, of which 1 were waited for; matrix products, arithmetic and copies ran while one was open for 1% of the time, Pallas kernels for 0%

commit v1 on v0

--- a/solution.py
+++ b/solution.py
@@ -91,7 +91,10 @@
     my_slash = lax.dynamic_slice_in_dim(slash, tp_pos * heads_loc, heads_loc, 0)
     first = seq_pos * block_list
     bids = first + jnp.arange(block_list, dtype=jnp.int32)
-    full = lax.all_gather(kv_rows, "seq", axis=0, tiled=True)
+    size = lax.axis_size("seq")
+    parts = jnp.stack([kv_rows for _ in range(size)])
+    parts = lax.all_to_all(parts, "seq", split_axis=0, concat_axis=0)
+    full = jnp.concatenate(parts, axis=0)
     index_table = full.reshape(full.shape[0] // BLK, BLK, kv_loc, 2 * HEAD_SIZE)
     front = 3 * block_list
     padded = jnp.concatenate(

time: 465 us -> 641 us (1.38)
  the two profiles are of different devices: /device:TPU:1 before, /device:TPU:216 now
where the time goes in v1:
time: 641 us; the launch traced here: 637 us
  waiting for transfers between devices  278 us (43%)
  loops' own time  135 us (21%)
  local copies, waits for them, and re-layouts  119 us (19%)
  other arithmetic  41.5 us (6%)
  matrix products  35.1 us (5%)
  blocking collectives  14.5 us (2%)
  starting transfers between devices  14 us (2%)
    all_to_all x1, waiting for transfers between devices, per_device(): parts = lax.all_to_all(parts, 'seq', split_axis=0, concat_axis=0)  278 us
    another operation x1, loops' own time, per_device(): outputs = lax.map(one_head, (qheads, my_vert, my_slash, owners))  135 us
    while x56, local copies, waits for them, and re-layouts  51.4 us
    gather x8, local copies, waits for them, and re-layouts, gather_rows(): vert_block = index_table[vertical_row, :, key_value_head]  32 us
    reduce_sum x8, other arithmetic, attend(): total = jnp.sum(weights, axis=(2, 3))  24.2 us
    all_to_all x1, blocking collectives, per_device(): lax.all_to_all(as_sent(attn), 'tp', split_axis=0, concat_axis=1, tiled=True)  14.5 us
    all_to_all x1, starting transfers between devices, per_device(): parts = lax.all_to_all(parts, 'seq', split_axis=0, concat_axis=0)  14 us
  transfers between devices with their start and end apart: 1, of which 1 were waited for; matrix products, arithmetic and copies ran while one was open for 0% of the time, Pallas kernels for 0%

profile of v1, /device:TPU:216, one launch (start us, length us, event | category | flops | bytes accessed | tf_op | source)
XLA Modules:
  0.0 636.7 jit_solution(8181299796096214101)
XLA Ops:
  0.0 5.1 stack.6
  5.2 14.0 %all-to-all-start = ((bf16[64,256,256]{2,1,0:T(8,128)(2,1)}), bf16[64,256,256]{2,1,0:T(8,128)(2,1)}, u32[]{:S(2)}, u32[]{:S(2)}) async-start(bf16[64,256,256]{2,1,0:T(8,128)(2,1)} %stack.6), calls=%async_computation | async-start | bytes 16777216 | tf_op jit(solution)/shard_map/all_to_all | solution.py:96
  19.6 0.9 copy.29
  20.6 277.5 %all-to-all-done = bf16[64,256,256]{2,1,0:T(8,128)(2,1)} async-done(((bf16[64,256,256]{2,1,0:T(8,128)(2,1)}), bf16[64,256,256]{2,1,0:T(8,128)(2,1)}, u32[]{:S(2)}, u32[]{:S(2)}) %all-to-all-start) | async-done | bytes 8388640 | tf_op jit(solution)/shard_map/all_to_all | solution.py:96
  298.1 8.4 %concatenate.19 = bf16[268,64,1,256]{3,1,0,2:T(8,128)(2,1)} pad(bf16[256,64,1,256]{3,1,0,2:T(8,128)(2,1)} %bitcast.1, bf16[]{:T(256)} %constant.98.clone.1), padding=12_0x0_0x0_0x0_0 | pad | bytes 17170434 | tf_op jit(solution)/shard_map/concatenate | solution.py:100
  306.6 313.2 %while.13 = (s32[]{:T(128)}, bf16[8,4,64,128]{3,2,1,0:T(8,128)(2,1)}, s32[8,32]{1,0:T(8,128)S(1)}, s32[8,8]{1,0:T(8,128)S(1)}, bf16[8,4,64,128]{3,2,1,0:T(8,128)...) while((s32[]{:T(128)}, ...), condition=%wide.region_4.5_spmd.clone, body=%wide.region_0.4_spmd.clone.sunk | while | flops 344332768 | bytes 21678552 | solution.py:117
  312.1 0.9 bitcast_dynamic-update-slice_fusion.17
  329.6 1.1 fusion.51
  333.6 4.0 gather_fusion
  337.6 1.6 fusion.53
  339.5 1.4 fusion.55
  341.0 3.0 fusion.56
  344.7 1.0 fusion.57
  351.3 0.9 bitcast_dynamic-update-slice_fusion.17
  368.8 1.1 fusion.51
  372.8 4.0 gather_fusion
  376.8 1.6 fusion.53
  378.7 1.4 fusion.55
  380.1 3.0 fusion.56
  383.9 1.0 fusion.57
  390.4 0.9 bitcast_dynamic-update-slice_fusion.17
  407.9 1.1 fusion.51
  412.0 4.0 gather_fusion
  416.0 1.6 fusion.53
  417.8 1.4 fusion.55
  419.3 3.0 fusion.56
  423.0 1.0 fusion.57
  429.6 0.9 bitcast_dynamic-update-slice_fusion.17
  447.1 1.1 fusion.51
  451.1 4.0 gather_fusion
  455.1 1.6 fusion.53
  457.0 1.4 fusion.55
  458.4 3.0 fusion.56
  462.2 1.0 fusion.57
  468.7 0.9 bitcast_dynamic-update-slice_fusion.17
  486.2 1.1 fusion.51
  490.3 4.0 gather_fusion
  494.3 1.6 fusion.53
  496.1 1.4 fusion.55
  497.6 3.0 fusion.56
  501.3 1.0 fusion.57
  507.9 0.9 bitcast_dynamic-update-slice_fusion.17
  525.4 1.1 fusion.51
  529.4 4.0 gather_fusion
  533.4 1.6 fusion.53
  535.3 1.4 fusion.55
  536.8 3.0 fusion.56
  540.5 1.0 fusion.57
  547.1 0.9 bitcast_dynamic-update-slice_fusion.17
  564.6 1.1 fusion.51
  568.6 4.0 gather_fusion
  572.6 1.6 fusion.53
  574.4 1.4 fusion.55
  575.9 3.0 fusion.56
  579.7 1.0 fusion.57
  586.2 0.9 bitcast_dynamic-update-slice_fusion.17
  603.7 1.1 fusion.51
  607.7 4.0 gather_fusion
  611.7 1.6 fusion.53
  613.6 1.4 fusion.55
  615.1 3.0 fusion.56
  618.8 1.0 fusion.57
  619.8 1.4 copy.31
  621.4 14.5 %all_to_all.24 = bf16[8,32,1024]{2,1,0:T(8,128)(2,1)S(1)} all-to-all(bf16[8,32,1024]{2,1,0:T(8,128)(2,1)S(1)} %all_to_all.18), channel_id=1, replica_groups=mesh['seq'=64,'tp'=8] {'tp'}, dimensions={0} | all-to-all | bytes 1048576 | tf_op jit(solution)/shard_map/all_to_all | solution.py:119
  (200 shorter events, 75.2 us)
Async XLA Ops:
  0.0 19.2 %copy-start = (s32[64,32]{0,1:T(8,128)S(1)}, s32[64,32]{0,1:T(8,128)}, u32[]{:S(2)}) copy-start(s32[64,32]{0,1:T(8,128)} %param.8) | copy-start | bytes 24580
  5.1 14.2 %copy-start.2 = (s32[64,8]{0,1:T(8,128)S(1)}, s32[64,8]{0,1:T(8,128)}, u32[]{:S(2)}) copy-start(s32[64,8]{0,1:T(8,128)} %param.9) | copy-start | bytes 6148
  5.2 14.3 %copy-start.1 = (bf16[256,1024]{1,0:T(8,128)(2,1)S(1)}, bf16[256,1024]{1,0:T(8,128)(2,1)}, u32[]{:S(2)}) copy-start(bf16[256,1024]{1,0:T(8,128)(2,1)} %param.6) | copy-start | bytes 1572868
  5.2 293.0 %all-to-all-start = ((bf16[64,256,256]{2,1,0:T(8,128)(2,1)}), bf16[64,256,256]{2,1,0:T(8,128)(2,1)}, u32[]{:S(2)}, u32[]{:S(2)}) async-start(bf16[64,256,256]{2,1,0:T(8,128)(2,1)} %stack.6), calls=%async_computation | async-start | bytes 16777216 | tf_op jit(solution)/shard_map/all_to_all | solution.py:96
